TPU v7x, 256 devices: a whole 4x4x8 slice. The times are simulated.
256 devices in a mesh: row: 8 (over x, y_hi), col: 32 (over z, y_lo, core).
Axes of the slice: x: 4, y: 4 (y_hi: 2, y_lo: 2; y = y_hi * 2 + y_lo), z: 8, core: 2. Of those that a mesh axis runs over, the one named last changes fastest.
Arguments:
- forward_state: bfloat16 [134217728], P(('row', 'col')), may hold values from -6 to 6
- adjoint_state: bfloat16 [134217728], P(('row', 'col')), may hold values from -6 to 6
- gate_matrix: bfloat16 [1024, 1024], replicated, may hold values from -1 to 1, as said below
Outputs:
- forward_final: bfloat16 [134217728], P(('row', 'col'))
- adjoint_final: bfloat16 [134217728], P(('row', 'col'))
- first_environment: float32 [1048576], P(('row', 'col'))
- second_environment: float32 [1048576], P(('row', 'col'))
Inputs may be any that keep to these rules, and one draw needn't show every extreme that they name: `gate_matrix`: an orthogonal matrix rounded to bfloat16.
All inputs are finite; a program needn't handle non-finite values.
Results may differ from a plain program's by a relative error of at most 0.0057.
Values may be sent and summed in bfloat16 or wider, within the bound.
A program may use at most 128 MiB of HBM per device.

v0:
```python
import math

import jax
import jax.numpy as jnp
from jax import lax
from jax.sharding import PartitionSpec as P


def swapped(value, axis, apart):
    return lax.ppermute(value, axis, [(i, i ^ 1 << apart) for i in range(lax.axis_size(axis))])


def trade_half(state, device_bit, position, sender):
    length = state.shape[0]
    halves = state.reshape(2**position, 2, length // 2 ** (position + 1))
    lower = halves[:, 0, :]
    upper = halves[:, 1, :]
    keep_lower = device_bit == 0
    outgoing = jnp.where(keep_lower, upper, lower)
    incoming = sender(outgoing)
    new_lower = jnp.where(keep_lower, lower, incoming)
    new_upper = jnp.where(keep_lower, incoming, upper)
    return jnp.stack([new_lower, new_upper], axis=1).reshape(length)


def advance(forward, adjoint, gate_matrix, scale):
    width = gate_matrix.shape[0]
    forward_blocks = forward.reshape(width, forward.shape[0] // width)
    adjoint_blocks = adjoint.reshape(width, adjoint.shape[0] // width)
    forward_moved = jnp.dot(gate_matrix, forward_blocks, preferred_element_type=jnp.float32).astype(
        jnp.bfloat16
    )
    adjoint_moved = jnp.dot(gate_matrix, adjoint_blocks, preferred_element_type=jnp.float32).astype(
        jnp.bfloat16
    )
    partial_env = (
        lax.dot_general(
            adjoint_moved,
            forward_blocks,
            (((1,), (1,)), ((), ())),
            preferred_element_type=jnp.float32,
        )
        * scale
    )
    return (forward_moved.reshape(-1), adjoint_moved.reshape(-1), partial_env.reshape(-1))


def on_device(forward_state, adjoint_state, gate_matrix):
    col_count = lax.axis_size("col")
    top_bit = col_count.bit_length() - 2
    col_index = lax.axis_index("col")
    row_value = lax.axis_index("row") % 2
    top_value = col_index // (col_count // 2) % 2
    low_value = col_index % 2
    scale = 1.0 / math.sqrt(
        lax.axis_size("row") * col_count * forward_state.shape[0] / gate_matrix.shape[0]
    )

    def row_trade(pair):
        return tuple(
            (trade_half(one, row_value, 0, lambda piece: swapped(piece, "row", 0)) for one in pair)
        )

    def col_trade(pair, bit_index, device_bit):
        return tuple(
            (
                trade_half(one, device_bit, 1, lambda piece: swapped(piece, "col", bit_index))
                for one in pair
            )
        )

    states = (forward_state, adjoint_state)
    states = row_trade(states)
    states = col_trade(states, top_bit, top_value)
    forward_now, adjoint_now, first_partial = advance(states[0], states[1], gate_matrix, scale)
    states = (forward_now, adjoint_now)
    first_environment = lax.psum_scatter(
        first_partial, ("row", "col"), scatter_dimension=0, tiled=True
    )
    states = row_trade(states)
    states = col_trade(states, top_bit, top_value)
    states = row_trade(states)
    states = col_trade(states, 0, low_value)
    forward_now, adjoint_now, second_partial = advance(states[0], states[1], gate_matrix, scale)
    states = (forward_now, adjoint_now)
    states = row_trade(states)
    states = col_trade(states, 0, low_value)
    second_environment = lax.psum_scatter(
        second_partial, ("row", "col"), scatter_dimension=0, tiled=True
    )
    return (states[0], states[1], first_environment, second_environment)


def solution(mesh):
    in_specs = (P(("row", "col")), P(("row", "col")), P())
    out_specs = (P(("row", "col")), P(("row", "col")), P(("row", "col")), P(("row", "col")))
    return jax.shard_map(
        on_device, mesh=mesh, in_specs=in_specs, out_specs=out_specs, check_vma=False
    )
```

profile of v0, /device:TPU:33, one launch (start us, length us, event | category | flops | bytes accessed | tf_op | source)
XLA Modules:
  0.0 552.4 jit_solution(7314425781156325595)
XLA Ops:
  11.5 2.9 collective-permute-start
  18.5 18.8 %collective-permute-done = bf16[1,262144]{1,0:T(2,128)(2,1)} collective-permute-done((bf16[1,262144]{1,0:T(2,128)(2,1)}, bf16[1,262144]{1,0:T(2,128)(2,1)}, u32[]{:S(2)}, u32[]{:S(2)}) %collective-permute-start) | collective-permute-done | bytes 524320 | tf_op jit(solution)/shard_map/ppermute | solution.py:10
  37.3 4.7 broadcast_select_fusion.22
  44.7 6.1 %collective-permute-start.1 = (bf16[2,131072]{1,0:T(2,128)(2,1)S(1)}, bf16[2,131072]{1,0:T(2,128)(2,1)S(1)}, u32[]{:S(2)}, u32[]{:S(2)}) collective-permute-start(bf16[2,131072]{1,0:T(2,128)(2,1)S(1)} %get-tuple-element.27), channel_id=1, source_target_pairs={{0,16},{1,17},{2,18},{3,19},{4,20},{5,21},{6,22},{7,23},{8,24},{9,... | collective-permute-start | bytes 1572872 | tf_op jit(solution)/shard_map/ppermute | solution.py:10
  50.8 9.1 %collective-permute-done.8 = bf16[1,262144]{1,0:T(2,128)(2,1)} collective-permute-done((bf16[1,262144]{1,0:T(2,128)(2,1)}, bf16[1,262144]{1,0:T(2,128)(2,1)}, u32[]{:S(2)}, u32[]{:S(2)}) %collective-permute-start.8) | collective-permute-done | bytes 524320 | tf_op jit(solution)/shard_map/ppermute | solution.py:10
  59.8 3.9 broadcast_select_fusion.10
  63.7 3.6 broadcast_select_fusion.29
  67.3 6.5 %collective-permute-start.9 = (bf16[2,131072]{1,0:T(2,128)(2,1)}, bf16[2,131072]{1,0:T(2,128)(2,1)}, u32[]{:S(2)}, u32[]{:S(2)}) collective-permute-start(bf16[2,131072]{1,0:T(2,128)(2,1)} %get-tuple-element.15), channel_id=1, source_target_pairs={{0,16},{1,17},{2,18},{3,19},{4,20},{5,21},{6,22},{7,23},{8,24},{9,... | collective-permute-start | bytes 1572872 | tf_op jit(solution)/shard_map/ppermute | solution.py:10
  87.6 3.1 collective-permute-start.2
  98.9 3.5 convolution_convert_fusion.1
  104.7 3.0 reshape_reshape.44
  107.7 3.2 broadcast_select_fusion.8
  112.6 3.0 copy.46
  115.6 3.9 broadcast_select_fusion.19
  122.2 4.4 collective-permute-start.3
  126.6 8.8 %collective-permute-done.10 = bf16[1,262144]{1,0:T(2,128)(2,1)S(1)} collective-permute-done((bf16[1,262144]{1,0:T(2,128)(2,1)S(1)}, bf16[1,262144]{1,0:T(2,128)(2,1)S(1)}, u32[]{:S(2)}, u32[]{:S(2)}) %collective-permute-start.10) | collective-permute-done | bytes 524320 | tf_op jit(solution)/shard_map/ppermute | solution.py:10
  135.4 2.9 broadcast_select_fusion.7
  148.3 19.0 %collective-permute-done.11 = bf16[2,131072]{1,0:T(2,128)(2,1)S(1)} collective-permute-done((bf16[2,131072]{1,0:T(2,128)(2,1)S(1)}, bf16[2,131072]{1,0:T(2,128)(2,1)S(1)}, u32[]{:S(2)}, u32[]{:S(2)}) %collective-permute-start.11) | collective-permute-done | bytes 524320 | tf_op jit(solution)/shard_map/ppermute | solution.py:10
  171.7 2.9 broadcast_select_fusion.16
  177.2 11.5 %collective-permute-start.5 = (bf16[2,131072]{1,0:T(2,128)(2,1)S(1)}, bf16[2,131072]{1,0:T(2,128)(2,1)S(1)}, u32[]{:S(2)}, u32[]{:S(2)}) collective-permute-start(bf16[2,131072]{1,0:T(2,128)(2,1)S(1)} %get-tuple-element.21), channel_id=1, source_target_pairs={{0,1},{1,0},{2,3},{3,2},{4,5},{5,4},{6,7},{7,6},{8,9},{9,8},{10,11... | collective-permute-start | bytes 1572872 | tf_op jit(solution)/shard_map/ppermute | solution.py:10
  188.7 2.9 broadcast_select_fusion.4
  191.5 3.6 broadcast_select_fusion.41
  195.2 10.2 %collective-permute-start.13 = (bf16[2,131072]{1,0:T(2,128)(2,1)}, bf16[2,131072]{1,0:T(2,128)(2,1)}, u32[]{:S(2)}, u32[]{:S(2)}) collective-permute-start(bf16[2,131072]{1,0:T(2,128)(2,1)} %get-tuple-element.9), channel_id=1, source_target_pairs={{0,1},{1,0},{2,3},{3,2},{4,5},{5,4},{6,7},{7,6},{8,9},{9,8},{10,11... | collective-permute-start | bytes 1572872 | tf_op jit(solution)/shard_map/ppermute | solution.py:10
  227.7 3.5 convolution_convert_fusion
  233.5 3.0 reshape_reshape.47
  236.5 4.0 broadcast_select_fusion.2
  240.4 3.3 collective-permute-start.14
  245.0 2.9 copy.47
  248.0 3.9 broadcast_select_fusion.13
  255.2 13.1 %collective-permute-done.14 = bf16[1,262144]{1,0:T(2,128)(2,1)} collective-permute-done((bf16[1,262144]{1,0:T(2,128)(2,1)}, bf16[1,262144]{1,0:T(2,128)(2,1)}, u32[]{:S(2)}, u32[]{:S(2)}) %collective-permute-start.14) | collective-permute-done | bytes 524320 | tf_op jit(solution)/shard_map/ppermute | solution.py:10
  268.3 3.9 broadcast_select_fusion.1
  285.2 257.5 %all-reduce.5.cloned.1.call-done = (f32[1048576]{0:T(1024)}, f32[1048576]{0:T(1024)}) async-done(((f32[1048576]{0:T(1024)}, f32[1048576]{0:T(1024)}), (f32[1048576]{0:T(1024)}, f32[1048576]{0:T(1024)})) %all-reduce.5.cloned.1.call-update) | async-done | bytes 8388624
  (99 shorter events, 101.2 us)
Async XLA Ops:
  7.2 71.9 %copy-start = (bf16[1024,1024]{1,0:T(8,128)(2,1)S(1)}, bf16[1024,1024]{1,0:T(8,128)(2,1)}, u32[]{:S(2)}) copy-start(bf16[1024,1024]{1,0:T(8,128)(2,1)} %param.5) | copy-start | bytes 6291460
  7.2 535.5 %all-reduce.5.cloned.1.call-start = ((), (), s32[]{:S(2)}) async-start(), calls=%async_computation | async-start | bytes 16777216
  8.9 2.6 copy-start.1
  11.5 25.9 %collective-permute-start = (bf16[1,262144]{1,0:T(2,128)(2,1)}, bf16[1,262144]{1,0:T(2,128)(2,1)}, u32[]{:S(2)}, u32[]{:S(2)}) collective-permute-start(bf16[1,262144]{1,0:T(2,128)(2,1)} %broadcast_select_fusion.23), channel_id=1, source_target_pairs={{0,32},{32,0},{64,96},{96,64},{128,160},{160,128},{192,224},{224,1... | collective-permute-start | bytes 1572872 | tf_op jit(solution)/shard_map/ppermute | solution.py:10
  18.5 41.3 %collective-permute-start.8 = (bf16[1,262144]{1,0:T(2,128)(2,1)}, bf16[1,262144]{1,0:T(2,128)(2,1)}, u32[]{:S(2)}, u32[]{:S(2)}) collective-permute-start(bf16[1,262144]{1,0:T(2,128)(2,1)} %broadcast_select_fusion.11), channel_id=1, source_target_pairs={{0,32},{32,0},{64,96},{96,64},{128,160},{160,128},{192,224},{224,1... | collective-permute-start | bytes 1572872 | tf_op jit(solution)/shard_map/ppermute | solution.py:10
  44.7 29.2 %collective-permute-start.1 = (bf16[2,131072]{1,0:T(2,128)(2,1)S(1)}, bf16[2,131072]{1,0:T(2,128)(2,1)S(1)}, u32[]{:S(2)}, u32[]{:S(2)}) collective-permute-start(bf16[2,131072]{1,0:T(2,128)(2,1)S(1)} %get-tuple-element.27), channel_id=1, source_target_pairs={{0,16},{1,17},{2,18},{3,19},{4,20},{5,21},{6,22},{7,23},{8,24},{9,... | collective-permute-start | bytes 1572872 | tf_op jit(solution)/shard_map/ppermute | solution.py:10
  67.3 23.3 %collective-permute-start.9 = (bf16[2,131072]{1,0:T(2,128)(2,1)}, bf16[2,131072]{1,0:T(2,128)(2,1)}, u32[]{:S(2)}, u32[]{:S(2)}) collective-permute-start(bf16[2,131072]{1,0:T(2,128)(2,1)} %get-tuple-element.15), channel_id=1, source_target_pairs={{0,16},{1,17},{2,18},{3,19},{4,20},{5,21},{6,22},{7,23},{8,24},{9,... | collective-permute-start | bytes 1572872 | tf_op jit(solution)/shard_map/ppermute | solution.py:10
  85.0 5.7 %copy-start.4 = (bf16[2,1,131072]{2,0,1:T(2,128)(2,1)S(1)}, bf16[2,1,131072]{2,0,1:T(2,128)(2,1)}, u32[]{:S(2)}) copy-start(bf16[2,1,131072]{2,0,1:T(2,128)(2,1)} %get-tuple-element.16) | copy-start | bytes 1572868
  85.0 5.7 %copy-start.5 = (bf16[2,131072]{1,0:T(2,128)(2,1)S(1)}, bf16[2,131072]{1,0:T(2,128)(2,1)}, u32[]{:S(2)}) copy-start(bf16[2,131072]{1,0:T(2,128)(2,1)} %get-tuple-element.17) | copy-start | bytes 1572868
  87.6 28.0 %collective-permute-start.2 = (bf16[1,262144]{1,0:T(2,128)(2,1)}, bf16[1,262144]{1,0:T(2,128)(2,1)}, u32[]{:S(2)}, u32[]{:S(2)}) collective-permute-start(bf16[1,262144]{1,0:T(2,128)(2,1)} %broadcast_select_fusion.20), channel_id=1, source_target_pairs={{0,32},{32,0},{64,96},{96,64},{128,160},{160,128},{192,224},{224,1... | collective-permute-start | bytes 1572872 | tf_op jit(solution)/shard_map/ppermute | solution.py:10
  107.7 3.6 copy-start.8
  107.7 3.6 copy-start.10
  110.9 24.4 %collective-permute-start.10 = (bf16[1,262144]{1,0:T(2,128)(2,1)S(1)}, bf16[1,262144]{1,0:T(2,128)(2,1)S(1)}, u32[]{:S(2)}, u32[]{:S(2)}) collective-permute-start(bf16[1,262144]{1,0:T(2,128)(2,1)S(1)} %broadcast_select_fusion.8), channel_id=1, source_target_pairs={{0,32},{32,0},{64,96},{96,64},{128,160},{160,128},{192,224},{224,1... | collective-permute-start | bytes 1572872 | tf_op jit(solution)/shard_map/ppermute | solution.py:10
  119.5 15.9 %copy-start.3 = (bf16[1,2,262144]{2,1,0:T(2,128)(2,1)S(1)}, bf16[1,2,262144]{2,1,0:T(2,128)(2,1)}, u32[]{:S(2)}) copy-start(bf16[1,2,262144]{2,1,0:T(2,128)(2,1)} %reshape_reshape.44) | copy-start | bytes 3145732
  122.2 19.2 %collective-permute-start.3 = (bf16[2,131072]{1,0:T(2,128)(2,1)S(1)}, bf16[2,131072]{1,0:T(2,128)(2,1)S(1)}, u32[]{:S(2)}, u32[]{:S(2)}) collective-permute-start(bf16[2,131072]{1,0:T(2,128)(2,1)S(1)} %get-tuple-element.24), channel_id=1, source_target_pairs={{0,16},{1,17},{2,18},{3,19},{4,20},{5,21},{6,22},{7,23},{8,24},{9,... | collective-permute-start | bytes 1572872 | tf_op jit(solution)/shard_map/ppermute | solution.py:10
  140.9 26.5 %collective-permute-start.11 = (bf16[2,131072]{1,0:T(2,128)(2,1)S(1)}, bf16[2,131072]{1,0:T(2,128)(2,1)S(1)}, u32[]{:S(2)}, u32[]{:S(2)}) collective-permute-start(bf16[2,131072]{1,0:T(2,128)(2,1)S(1)} %get-tuple-element.12), channel_id=1, source_target_pairs={{0,16},{1,17},{2,18},{3,19},{4,20},{5,21},{6,22},{7,23},{8,24},{9,... | collective-permute-start | bytes 1572872 | tf_op jit(solution)/shard_map/ppermute | solution.py:10
  145.6 26.0 %collective-permute-start.4 = (bf16[1,262144]{1,0:T(2,128)(2,1)S(1)}, bf16[1,262144]{1,0:T(2,128)(2,1)S(1)}, u32[]{:S(2)}, u32[]{:S(2)}) collective-permute-start(bf16[1,262144]{1,0:T(2,128)(2,1)S(1)} %broadcast_select_fusion.17), channel_id=1, source_target_pairs={{0,32},{32,0},{64,96},{96,64},{128,160},{160,128},{192,224},{224,1... | collective-permute-start | bytes 1572872 | tf_op jit(solution)/shard_map/ppermute | solution.py:10
  171.6 17.1 %collective-permute-start.12 = (bf16[1,262144]{1,0:T(2,128)(2,1)S(1)}, bf16[1,262144]{1,0:T(2,128)(2,1)S(1)}, u32[]{:S(2)}, u32[]{:S(2)}) collective-permute-start(bf16[1,262144]{1,0:T(2,128)(2,1)S(1)} %broadcast_select_fusion.5), channel_id=1, source_target_pairs={{0,32},{32,0},{64,96},{96,64},{128,160},{160,128},{192,224},{224,1... | collective-permute-start | bytes 1572872 | tf_op jit(solution)/shard_map/ppermute | solution.py:10
  177.2 28.2 %collective-permute-start.5 = (bf16[2,131072]{1,0:T(2,128)(2,1)S(1)}, bf16[2,131072]{1,0:T(2,128)(2,1)S(1)}, u32[]{:S(2)}, u32[]{:S(2)}) collective-permute-start(bf16[2,131072]{1,0:T(2,128)(2,1)S(1)} %get-tuple-element.21), channel_id=1, source_target_pairs={{0,1},{1,0},{2,3},{3,2},{4,5},{5,4},{6,7},{7,6},{8,9},{9,8},{10,11... | collective-permute-start | bytes 1572872 | tf_op jit(solution)/shard_map/ppermute | solution.py:10
  195.2 24.2 %collective-permute-start.13 = (bf16[2,131072]{1,0:T(2,128)(2,1)}, bf16[2,131072]{1,0:T(2,128)(2,1)}, u32[]{:S(2)}, u32[]{:S(2)}) collective-permute-start(bf16[2,131072]{1,0:T(2,128)(2,1)} %get-tuple-element.9), channel_id=1, source_target_pairs={{0,1},{1,0},{2,3},{3,2},{4,5},{5,4},{6,7},{7,6},{8,9},{9,8},{10,11... | collective-permute-start | bytes 1572872 | tf_op jit(solution)/shard_map/ppermute | solution.py:10
  216.5 2.9 copy-start.6
  216.5 2.9 copy-start.7
  219.1 28.9 %collective-permute-start.6 = (bf16[1,262144]{1,0:T(2,128)(2,1)}, bf16[1,262144]{1,0:T(2,128)(2,1)}, u32[]{:S(2)}, u32[]{:S(2)}) collective-permute-start(bf16[1,262144]{1,0:T(2,128)(2,1)} %broadcast_select_fusion.14), channel_id=1, source_target_pairs={{0,32},{32,0},{64,96},{96,64},{128,160},{160,128},{192,224},{224,1... | collective-permute-start | bytes 1572872 | tf_op jit(solution)/shard_map/ppermute | solution.py:10
  236.5 7.2 %copy-start.9 = (bf16[1024,512]{1,0:T(8,128)(2,1)S(1)}, bf16[1024,512]{1,0:T(8,128)(2,1)}, u32[]{:S(2)}) copy-start(bf16[1024,512]{1,0:T(8,128)(2,1)} %reshape_reshape.41) | copy-start | bytes 3145732
  236.5 7.2 %copy-start.11 = (bf16[512,1024]{1,0:T(8,128)(2,1)S(1)}, bf16[512,1024]{1,0:T(8,128)(2,1)}, u32[]{:S(2)}) copy-start(bf16[512,1024]{1,0:T(8,128)(2,1)} %convolution_convert_fusion) | copy-start | bytes 3145732
  240.4 27.8 %collective-permute-start.14 = (bf16[1,262144]{1,0:T(2,128)(2,1)}, bf16[1,262144]{1,0:T(2,128)(2,1)}, u32[]{:S(2)}, u32[]{:S(2)}) collective-permute-start(bf16[1,262144]{1,0:T(2,128)(2,1)} %broadcast_select_fusion.2), channel_id=1, source_target_pairs={{0,32},{32,0},{64,96},{96,64},{128,160},{160,128},{192,224},{224,1... | collective-permute-start | bytes 1572872 | tf_op jit(solution)/shard_map/ppermute | solution.py:10
  251.9 16.4 %copy-start.2 = (bf16[1,2,262144]{2,1,0:T(2,128)(2,1)S(1)}, bf16[1,2,262144]{2,1,0:T(2,128)(2,1)}, u32[]{:S(2)}) copy-start(bf16[1,2,262144]{2,1,0:T(2,128)(2,1)} %reshape_reshape.47) | copy-start | bytes 3145732
  254.6 21.4 %collective-permute-start.7 = (bf16[2,131072]{1,0:T(2,128)(2,1)S(1)}, bf16[2,131072]{1,0:T(2,128)(2,1)S(1)}, u32[]{:S(2)}, u32[]{:S(2)}) collective-permute-start(bf16[2,131072]{1,0:T(2,128)(2,1)S(1)} %get-tuple-element.18), channel_id=1, source_target_pairs={{0,1},{1,0},{2,3},{3,2},{4,5},{5,4},{6,7},{7,6},{8,9},{9,8},{10,11... | collective-permute-start | bytes 1572872 | tf_op jit(solution)/shard_map/ppermute | solution.py:10
  274.9 3.5 collective-permute-start.15
Sparse Core Ops, SparseCore 0:
  248.1 294.5 all-reduce.4
where the time goes:
time: 563 us; the launch traced here: 552 us
  waiting for transfers between devices  326 us (58%)
  other arithmetic  94.4 us (17%)
  starting transfers between devices  53.7 us (10%)
  local copies, waits for them, and re-layouts  48.6 us (9%)
  matrix products  14.7 us (3%)
  between operations  14.7 us (3%)
    unnamed x2, waiting for transfers between devices  258 us
    ppermute x16, waiting for transfers between devices, swapped(): lax.ppermute(value, axis, [(i, i ^ 1 << apart) for i in range(lax.axis_si...  68.8 us
    ppermute x16, starting transfers between devices, swapped(): lax.ppermute(value, axis, [(i, i ^ 1 << apart) for i in range(lax.axis_si...  53.7 us
    select_n x16, other arithmetic, trade_half(): outgoing = jnp.where(keep_lower, upper, lower)  44.1 us
    select_n x8, other arithmetic, trade_half(): new_lower = jnp.where(keep_lower, lower, incoming)  28.9 us
    another operation x16, other arithmetic, trade_half(): return jnp.stack([new_lower, new_upper], axis=1).reshape(length)  21.3 us
  transfers between devices with their start and end apart: 17, of which 6 were waited for; matrix products, arithmetic and copies ran while one was open for 27% of the time, Pallas kernels for 0%

commit v1 on v0

v1 whole, which is shorter than its diff:
```python
import math

import jax
import jax.numpy as jnp
from jax import lax
from jax.experimental import pallas as pl
from jax.experimental.pallas import tpu as pltpu
from jax.sharding import PartitionSpec as P

MESH = pl.DeviceIdType.MESH
BF = jnp.bfloat16
F32 = jnp.float32


def flip(bit, by):
    return 1 - bit if by else bit


def kernel(
    scale, f_in, a_in, g_in, f_out, a_out, e1_out, e2_out,
    gate, flat, tmp, x1, x2, sb, fin, acc, cs, cr, xs, xr, yb, yr, zb, zr, fb, lc, lr,
    load_sem, home_sem, ex_s, ex_r, co_s, co_r, fi_s, fi_r, cs_s, cs_r, xs_s, xs_r, ys_s, ys_r, zs_s, zs_r, lc_s, lc_r,
):
    row, col = lax.axis_index("row"), lax.axis_index("col")
    xa, xb, yh = lax.div(row, 4), lax.rem(lax.div(row, 2), 2), lax.rem(row, 2)
    zh, zm, zl = lax.div(col, 16), lax.rem(lax.div(col, 8), 2), lax.rem(lax.div(col, 4), 2)
    yl, k = lax.rem(lax.div(col, 2), 2), lax.rem(col, 2)
    oth = 1 - k

    def peer(dx=0, dy=0, dz=0, dk=0):
        return {
            "row": (flip(xa, dx & 2) * 2 + flip(xb, dx & 1)) * 2 + flip(yh, dy & 2),
            "col": ((flip(zh, dz & 4) * 2 + flip(zm, dz & 2)) * 2 + flip(zl, dz & 1)) * 4
            + flip(yl, dy & 1) * 2
            + flip(k, dk),
        }

    def remote(src, dst, send, recv, to):
        return pltpu.make_async_remote_copy(
            src_ref=src, dst_ref=dst, send_sem=send, recv_sem=recv, device_id=to, device_id_type=MESH
        )

    ins, outs, env_outs = (f_in, a_in), (f_out, a_out), (e1_out, e2_out)
    home = yh * 2 + zh

    group = [(r, c, d) for r in (0, 1) for c in (1, 0) for d in (0, 1) if r + c + d]
    friends = [peer(dy=2 * r, dz=4 * c, dk=d) for r, c, d in group]
    friends += [peer(dx=d) for d in (1, 2, 3)] + [peer(dy=d) for d in (1, 3)]
    friends += [peer(dz=d) for d in (1, 2, 3, 5, 6, 7)]
    barrier = pltpu.get_barrier_semaphore()
    for friend in friends:
        pl.semaphore_signal(barrier, inc=1, device_id=friend, device_id_type=MESH)

    loads = [pltpu.make_async_copy(g_in, gate, load_sem.at[2])]
    for s in (0, 1):
        loads.append(pltpu.make_async_copy(ins[s].at[home], flat.at[s, home], load_sem.at[s]))
    for one in loads:
        one.start()
    pl.semaphore_wait(barrier, len(friends))

    steps = ((0, 1), (1, 1), (1, 0))
    first = {}
    for s in (0, 1):
        for j, (r, c) in enumerate(steps):
            quarter = flip(yh, r) * 2 + flip(zh, c)
            first[s, j] = remote(
                ins[s].at[quarter], flat.at[s, home], ex_s.at[s, j], ex_r.at[s, j], peer(dy=2 * r, dz=4 * c)
            )
            first[s, j].start()

    def untangle(s, slot):
        tmp[...] = flat[s, slot].astype(F32)
        rows = pl.ds(pl.multiple_of(slot * 256, 256), 256)
        for m in range(4):
            x1[s, m // 2, rows, (m % 2) * 128 : (m % 2) * 128 + 128] = tmp[pl.ds(m, 256, stride=4), :].astype(BF)

    def gather(s):
        loads[1 + s].wait()
        untangle(s, home)
        for j in (2, 0, 1):
            r, c = steps[j]
            first[s, j].wait_recv()
            untangle(s, flip(yh, r) * 2 + flip(zh, c))

    def block(i):
        return pl.ds(pl.multiple_of(i * 256, 256), 256)

    swaps = {}

    def gate_one(s):
        def other(i, carry):
            sb[s, i] = jnp.dot(gate[block(i), :], x1[s, oth], preferred_element_type=F32).astype(BF)
            return carry

        lax.fori_loop(0, 4, other, 0)
        for i in range(4):
            swaps[s, i] = remote(
                sb.at[s, i],
                x2.at[s, i % 2, block((i // 2) * 2 + k), :],
                co_s.at[s, i],
                co_r.at[s, i],
                peer(dk=1),
            )
            swaps[s, i].start()

        def own(i, carry):
            x2[s, lax.rem(i, 2), block(lax.div(i, 2) * 2 + k), :] = jnp.dot(
                gate[block(i), :], x1[s, k], preferred_element_type=F32
            ).astype(BF)
            return carry

        lax.fori_loop(0, 4, own, 0)

    last, homes = {}, []

    def gate_two(s):
        for i in range(4):
            swaps[s, i].wait_recv()
        for c in (1, 0):
            top = flip(zh, c)

            def apply(i, carry):
                fin[s, top, block(i), :] = jnp.dot(
                    gate[block(i), :], x2[s, top], preferred_element_type=F32
                ).astype(BF)
                return carry

            lax.fori_loop(0, 4, apply, 0)
            for r in (1, 0):
                for d in (0, 1):
                    src = fin.at[s, top, block(flip(yh, r) * 2 + flip(k, d)), :]
                    dst = outs[s].at[home, :, block(k)]
                    if r + c + d == 0:
                        one = pltpu.make_async_copy(src, dst, home_sem.at[s])
                        homes.append(one)
                    else:
                        j = group.index((r, c, d))
                        one = remote(src, dst, fi_s.at[s, j], fi_r.at[s, j], peer(dy=2 * r, dz=4 * c, dk=d))
                        last[s, j] = one
                    one.start()

    def outer(a, b):
        return lax.dot_general(a, b, (((1,), (1,)), ((), ())), preferred_element_type=F32)

    pairs = {}

    def half(i):
        return pl.ds(pl.multiple_of(i * 512, 512), 512)

    def env_blocks(e, left, right):
        def one(t, carry):
            d = lax.rem(t + 1, 4)
            da, db = lax.div(d, 2), lax.rem(d, 2)
            ia, ib = xa + da - 2 * xa * da, xb + db - 2 * xb * db
            lo, hi = left(ia, ib)
            cs[e, d] = (outer(lo, right(0, oth)) + outer(hi, right(1, oth))).astype(BF)
            acc[e, d] = outer(lo, right(0, k)) + outer(hi, right(1, k))
            return carry

        lax.fori_loop(0, 4, one, 0)
        for d in (1, 2, 3, 0):
            pairs[e, d] = remote(cs.at[e, d], cr.at[e, d], cs_s.at[e, d], cs_r.at[e, d], peer(dk=1))
            pairs[e, d].start()

    def env_one():
        env_blocks(
            0,
            lambda ia, ib: (sb[1, ia * 2 + ib], x2[1, ib, block(ia * 2 + k), :]),
            lambda m, h: x1[0, oth if m == 0 else k, half(h), :],
        )

    def env_two():
        env_blocks(
            1,
            lambda ia, ib: (fin[1, 0, block(ia * 2 + ib), :], fin[1, 1, block(ia * 2 + ib), :]),
            lambda m, h: x2[0, m, half(h), :],
        )

    xsend, ysend, zsend, csend = {}, {}, {}, {}

    def stage_x(e):
        for d in (1, 2, 3):
            pairs[e, d].wait_recv()
            xs[e, d - 1] = (acc[e, d] + cr[e, d].astype(F32)).astype(BF)
            xsend[e, d] = remote(xs.at[e, d - 1], xr.at[e, d - 1], xs_s.at[e, d - 1], xs_r.at[e, d - 1], peer(dx=d))
            xsend[e, d].start()
        pairs[e, 0].wait_recv()

    def stage_y(e):
        for d in (1, 2, 3):
            xsend[e, d].wait_recv()

        def gather_rows(t, carry):
            rows = pl.ds(pl.multiple_of(t * 16, 16), 16)
            total = acc[e, 0, rows, :] + cr[e, 0, rows, :].astype(F32)
            for j in range(3):
                total = total + xr[e, j, rows, :].astype(F32)
            y, z = lax.div(t, 8), lax.rem(t, 8)
            yb[e, y * 2, z] = total[:8]
            yb[e, y * 2 + 1, z] = total[8:]
            return carry

        lax.fori_loop(0, 16, gather_rows, 0)
        for d in (2, 1, 3):
            ysend[e, d] = remote(
                yb.at[e, flip(yh, d & 2) * 2 + flip(yl, d & 1)],
                yr.at[e, d - 1],
                ys_s.at[e, d - 1],
                ys_r.at[e, d - 1],
                peer(dy=d),
            )
            ysend[e, d].start()

    def stage_z(e):
        for d in (1, 2, 3):
            ysend[e, d].wait_recv()
        zb[e] = yb[e, yh * 2 + yl] + yr[e, 0] + yr[e, 1] + yr[e, 2]
        for d in (4, 5, 3, 6, 2, 7, 1):
            zsend[e, d] = remote(
                zb.at[e, (flip(zh, d & 4) * 2 + flip(zm, d & 2)) * 2 + flip(zl, d & 1)],
                zr.at[e, d - 1],
                zs_s.at[e, d - 1],
                zs_r.at[e, d - 1],
                peer(dz=d),
            )
            zsend[e, d].start()

    def stage_core(e):
        for d in range(1, 8):
            zsend[e, d].wait_recv()
        total = zb[e, (zh * 2 + zm) * 2 + zl]
        for d in range(7):
            total = total + zr[e, d]
        for j in range(4):
            fb[e, j * 8 : j * 8 + 8, :] = total[:, j * 128 : j * 128 + 128] * scale
        for j in range(4):
            lc[e, j * 4 : j * 4 + 4, :] = fb[e, pl.ds(j * 8 + oth * 4, 4), :]
            env_outs[e][pl.ds(k * 4 + j, 4, stride=8), :] = fb[e, pl.ds(j * 8 + k * 4, 4), :]
        csend[e] = remote(lc.at[e], lr.at[e], lc_s.at[e], lc_r.at[e], peer(dk=1))
        csend[e].start()

    def stage_end(e):
        csend[e].wait_recv()
        for j in range(4):
            env_outs[e][pl.ds(oth * 4 + j, 4, stride=8), :] = lr[e, j * 4 : j * 4 + 4, :]

    loads[0].wait()
    gather(0)
    gate_one(0)
    gate_two(0)
    gather(1)
    gate_one(1)
    env_one()
    gate_two(1)
    env_two()
    stage_x(0)
    stage_x(1)
    stage_y(0)
    stage_z(0)
    stage_y(1)
    stage_z(1)
    stage_core(0)
    stage_core(1)
    stage_end(0)
    stage_end(1)
    for one in last.values():
        one.wait_recv()
    for one in homes:
        one.wait()
    for sent in (first, swaps, last, pairs, xsend, ysend, zsend, csend):
        for one in sent.values():
            one.wait_send()


def on_device(forward_state, adjoint_state, gate_matrix):
    scale = 1.0 / math.sqrt(lax.axis_size("row") * lax.axis_size("col") * forward_state.shape[0] / gate_matrix.shape[0])
    dma = pltpu.SemaphoreType.DMA
    any_space = pl.BlockSpec(memory_space=pl.ANY)
    vmem = pl.BlockSpec(memory_space=pltpu.VMEM)
    scratch = [
        ((1024, 1024), BF),
        ((2, 4, 1024, 128), BF),
        ((1024, 128), F32),
        ((2, 2, 1024, 256), BF),
        ((2, 2, 1024, 256), BF),
        ((2, 4, 256, 256), BF),
        ((2, 2, 1024, 256), BF),
        ((2, 4, 256, 512), F32),
        ((2, 4, 256, 512), BF),
        ((2, 4, 256, 512), BF),
        ((2, 3, 256, 512), BF),
        ((2, 3, 256, 512), BF),
        ((2, 4, 8, 8, 512), F32),
        ((2, 3, 8, 8, 512), F32),
        ((2, 8, 8, 512), F32),
        ((2, 7, 8, 512), F32),
        ((2, 32, 128), F32),
        ((2, 16, 128), F32),
        ((2, 16, 128), F32),
    ]
    sems = [(3,), (2,)]
    for shape in ((2, 3), (2, 4), (2, 7), (2, 4), (2, 3), (2, 3), (2, 7), (2,)):
        sems += [shape, shape]
    outs = pl.pallas_call(
        lambda *refs: kernel(scale, *refs),
        out_shape=[
            jax.ShapeDtypeStruct((4, 256, 512), BF),
            jax.ShapeDtypeStruct((4, 256, 512), BF),
            jax.ShapeDtypeStruct((32, 128), F32),
            jax.ShapeDtypeStruct((32, 128), F32),
        ],
        in_specs=[any_space] * 3,
        out_specs=[any_space, any_space, vmem, vmem],
        scratch_shapes=[pltpu.VMEM(shape, kind) for shape, kind in scratch] + [dma(shape) for shape in sems],
        compiler_params=pltpu.CompilerParams(collective_id=0, has_side_effects=True),
        name="step",
    )(forward_state.reshape(4, 1024, 128), adjoint_state.reshape(4, 1024, 128), gate_matrix)
    return tuple(one.reshape(-1) for one in outs)


def solution(mesh):
    spec = P(("row", "col"))
    return jax.shard_map(
        on_device, mesh=mesh, in_specs=(spec, spec, P()), out_specs=(spec, spec, spec, spec), check_vma=False
    )
```

time: 563 us -> 136 us (0.24); the launches traced: 552 us -> 135 us
  waiting for transfers between devices: 326 us -> 0 us
  Pallas kernels: 0 us -> 129 us
  other arithmetic: 94.4 us -> 0 us
  starting transfers between devices: 53.7 us -> 0 us
  local copies, waits for them, and re-layouts: 48.6 us -> 5.31 us
  matrix products: 14.7 us -> 0 us
  between operations: 14.7 us -> 0.67 us
    unnamed x2 -> x0, waiting for transfers between devices: 258 us -> none
    pallas_call x0 -> x1, Pallas kernels: none -> 129 us  [on_device(): pl.pallas_call(lambda *refs: kernel(scale, *refs), out_shape=[jax.ShapeDt...]
    select_n x24 -> x0, other arithmetic: 73.1 us -> none  [the longest x16 44.1 us: trade_half(): outgoing = jnp.where(keep_lower, upper, lower)]
    ppermute x16 -> x0, waiting for transfers between devices: 68.8 us -> none  [swapped(): lax.ppermute(value, axis, [(i, i ^ 1 << apart) for i in range(lax.axis_si...]
    ppermute x16 -> x0, starting transfers between devices: 53.7 us -> none  [swapped(): lax.ppermute(value, axis, [(i, i ^ 1 << apart) for i in range(lax.axis_si...]
    another operation x14 -> x0, local copies, waits for them, and re-layouts: 27.5 us -> none  [the longest x4 9.98 us: trade_half(): halves = state.reshape(2 ** position, 2, length // 2 ** (position + 1))]
    another operation x16 -> x0, other arithmetic: 21.3 us -> none  [trade_half(): return jnp.stack([new_lower, new_upper], axis=1).reshape(length)]
    dot_general x6 -> x0, matrix products: 14.7 us -> none  [the longest x2 7.03 us: advance(): jnp.dot(gate_matrix, adjoint_blocks, preferred_element_type=jnp.float32)]
  transfers between devices with their start and end apart: 17 -> 0, of which waited for: 6 -> 0; matrix products, arithmetic and copies ran while one was open for 27% -> 0% of each run, Pallas kernels for 0% -> 0%
where the time goes in v1:
time: 136 us; the launch traced here: 135 us
  Pallas kernels  129 us (95%)
  local copies, waits for them, and re-layouts  5.31 us (4%)
    pallas_call x1, Pallas kernels, on_device(): pl.pallas_call(lambda *refs: kernel(scale, *refs), out_shape=[jax.ShapeDt...  129 us
    unnamed x10, local copies, waits for them, and re-layouts  5.31 us

profile of v1, /device:TPU:33, one launch (start us, length us, event | category | flops | bytes accessed | tf_op | source)
XLA Modules:
  0.0 134.7 jit_solution(9731206628657466812)
XLA Ops:
  0.6 128.7 %step.1 = (bf16[4,256,512]{2,1,0:T(8,128)(2,1)}, bf16[4,256,512]{2,1,0:T(8,128)(2,1)}, f32[32,128]{1,0:T(8,128)}, f32[32,128]{1,0:T(8,128)}) custom-call(bf16[4,1024,128]{2,1,0:T(8,128)(2,1)} %bitcast.12, bf16[4,1024,128]{2,1,0:T(8,128)(2,1)} %bitcast.13, bf16[1024,1024]{1,0:T(8,128)(2,1)} %refs_2_.1), custom_call_target="tpu_custom_call" | custom-call | tf_op jit(solution)/shard_map/step/pallas_call | solution.py:304
  129.4 0.0 copy-start
  129.4 0.0 copy-start.2
  129.4 0.0 copy-start.1
  129.4 2.7 %copy.7 = bf16[128,4,8,128]{3,1,2,0:T(4,128)(2,1)} copy(bf16[128,4,8,128]{3,2,1,0:T(8,128)(2,1)} %bitcast.11) | data formatting | bytes 2097152
  132.1 0.0 copy-done
  132.1 1.4 %copy.8 = bf16[128,4,8,128]{3,1,2,0:T(4,128)(2,1)} copy(bf16[128,4,8,128]{3,2,1,0:T(8,128)(2,1)S(1)} %bitcast.10) | data formatting | bytes 2097152
  133.5 0.0 copy-done.2
  133.5 0.6 copy.11
  134.1 0.0 copy-done.1
  134.1 0.6 copy.12
Async XLA Ops:
  129.4 2.7 %copy-start = (bf16[4,256,512]{2,1,0:T(8,128)(2,1)S(1)}, bf16[4,256,512]{2,1,0:T(8,128)(2,1)}, u32[]{:S(2)}) copy-start(bf16[4,256,512]{2,1,0:T(8,128)(2,1)} %get-tuple-element.9) | copy-start | bytes 3145732
  129.4 4.1 %copy-start.2 = (f32[32,128]{1,0:T(8,128)S(1)}, f32[32,128]{1,0:T(8,128)}, u32[]{:S(2)}) copy-start(f32[32,128]{1,0:T(8,128)} %get-tuple-element.10) | copy-start | bytes 49156
  129.4 4.7 %copy-start.1 = (f32[32,128]{1,0:T(8,128)S(1)}, f32[32,128]{1,0:T(8,128)}, u32[]{:S(2)}) copy-start(f32[32,128]{1,0:T(8,128)} %get-tuple-element.11) | copy-start | bytes 49156

commit v2 on v1

--- a/solution.py
+++ b/solution.py
@@ -18,8 +18,9 @@
 
 def kernel(
     scale, f_in, a_in, g_in, f_out, a_out, e1_out, e2_out,
-    gate, flat, tmp, x1, x2, sb, fin, acc, cs, cr, xs, xr, yb, yr, zb, zr, fb, lc, lr,
-    load_sem, home_sem, ex_s, ex_r, co_s, co_r, fi_s, fi_r, cs_s, cs_r, xs_s, xs_r, ys_s, ys_r, zs_s, zs_r, lc_s, lc_r,
+    gate, flat, legs, legs2, tmp, x1, x2, sb, fin, ac0, ac1, mid, cs, cr, xs, xr, ys, yr, ys2, yr2, xs2, xr2, zb, zs, zr, fb, lc, lr,
+    load_sem, home_sem, ex_s, ex_r, le_s, le_r, le2_s, le2_r, co_s, co_r, fi_s, fi_r, cs_s, cs_r, xs_s, xs_r, ys_s, ys_r,
+    ys2_s, ys2_r, xs2_s, xs2_r, zs_s, zs_r, lc_s, lc_r,
 ):
     row, col = lax.axis_index("row"), lax.axis_index("col")
     xa, xb, yh = lax.div(row, 4), lax.rem(lax.div(row, 2), 2), lax.rem(row, 2)
@@ -59,14 +60,35 @@
     pl.semaphore_wait(barrier, len(friends))
 
     steps = ((0, 1), (1, 1), (1, 0))
-    first = {}
-    for s in (0, 1):
-        for j, (r, c) in enumerate(steps):
-            quarter = flip(yh, r) * 2 + flip(zh, c)
-            first[s, j] = remote(
-                ins[s].at[quarter], flat.at[s, home], ex_s.at[s, j], ex_r.at[s, j], peer(dy=2 * r, dz=4 * c)
-            )
-            first[s, j].start()
+    first, relays = {}, {}
+
+    def quarter(r, c):
+        return flip(yh, r) * 2 + flip(zh, c)
+
+    def open_leg(s):
+        relays[s] = remote(ins[s].at[quarter(1, 1)], legs.at[s], le_s.at[s], le_r.at[s], peer(dy=2))
+        relays[s].start()
+
+    def open_direct(s, j):
+        r, c = steps[j]
+        first[s, j] = remote(
+            ins[s].at[quarter(r, c)], flat.at[s, home], ex_s.at[s, j], ex_r.at[s, j], peer(dy=2 * r, dz=4 * c)
+        )
+        first[s, j].start()
+
+    def open_relay(s):
+        relays[s].wait_recv()
+        first[s, 1] = remote(legs.at[s], flat.at[s, quarter(1, 0)], ex_s.at[s, 1], ex_r.at[s, 1], peer(dz=4))
+        first[s, 1].start()
+
+    open_direct(0, 0)
+    open_leg(0)
+    open_leg(1)
+    open_direct(0, 2)
+    open_direct(1, 2)
+    open_relay(0)
+    open_direct(1, 0)
+    open_relay(1)
 
     def untangle(s, slot):
         tmp[...] = flat[s, slot].astype(F32)
@@ -74,13 +96,13 @@
         for m in range(4):
             x1[s, m // 2, rows, (m % 2) * 128 : (m % 2) * 128 + 128] = tmp[pl.ds(m, 256, stride=4), :].astype(BF)
 
-    def gather(s):
-        loads[1 + s].wait()
-        untangle(s, home)
-        for j in (2, 0, 1):
-            r, c = steps[j]
+    def gather(s, j):
+        if j < 0:
+            loads[1 + s].wait()
+            untangle(s, home)
+        else:
             first[s, j].wait_recv()
-            untangle(s, flip(yh, r) * 2 + flip(zh, c))
+            untangle(s, quarter(*steps[j]))
 
     def block(i):
         return pl.ds(pl.multiple_of(i * 256, 256), 256)
@@ -111,33 +133,51 @@
 
         lax.fori_loop(0, 4, own, 0)
 
-    last, homes = {}, []
-
-    def gate_two(s):
+    last, relays2, homes = {}, {}, []
+
+    def piece(s, r, c, d):
+        return fin.at[s, flip(zh, c), block(flip(yh, r) * 2 + flip(k, d)), :]
+
+    def close_leg(s):
+        for d in (0, 1):
+            relays2[s, d] = remote(piece(s, 1, 1, d), legs2.at[s, d], le2_s.at[s, d], le2_r.at[s, d], peer(dy=2))
+            relays2[s, d].start()
+
+    def close(s, r, c, d):
+        dst = outs[s].at[home, :, block(k)]
+        if r + c + d == 0:
+            one = pltpu.make_async_copy(piece(s, r, c, d), dst, home_sem.at[s])
+            homes.append(one)
+        else:
+            j = group.index((r, c, d))
+            one = remote(piece(s, r, c, d), dst, fi_s.at[s, j], fi_r.at[s, j], peer(dy=2 * r, dz=4 * c, dk=d))
+            last[s, j] = one
+        one.start()
+
+    def close_relay(s, d):
+        j = group.index((1, 1, d))
+        relays2[s, d].wait_recv()
+        last[s, j] = remote(
+            legs2.at[s, d],
+            outs[s].at[quarter(1, 0), :, block(k)],
+            fi_s.at[s, j],
+            fi_r.at[s, j],
+            peer(dz=4, dk=d),
+        )
+        last[s, j].start()
+
+    def gate_two(s, c):
+        top = flip(zh, c)
+
+        def apply(i, carry):
+            fin[s, top, block(i), :] = jnp.dot(gate[block(i), :], x2[s, top], preferred_element_type=F32).astype(BF)
+            return carry
+
+        lax.fori_loop(0, 4, apply, 0)
+
+    def swapped(s):
         for i in range(4):
             swaps[s, i].wait_recv()
-        for c in (1, 0):
-            top = flip(zh, c)
-
-            def apply(i, carry):
-                fin[s, top, block(i), :] = jnp.dot(
-                    gate[block(i), :], x2[s, top], preferred_element_type=F32
-                ).astype(BF)
-                return carry
-
-            lax.fori_loop(0, 4, apply, 0)
-            for r in (1, 0):
-                for d in (0, 1):
-                    src = fin.at[s, top, block(flip(yh, r) * 2 + flip(k, d)), :]
-                    dst = outs[s].at[home, :, block(k)]
-                    if r + c + d == 0:
-                        one = pltpu.make_async_copy(src, dst, home_sem.at[s])
-                        homes.append(one)
-                    else:
-                        j = group.index((r, c, d))
-                        one = remote(src, dst, fi_s.at[s, j], fi_r.at[s, j], peer(dy=2 * r, dz=4 * c, dk=d))
-                        last[s, j] = one
-                    one.start()
 
     def outer(a, b):
         return lax.dot_general(a, b, (((1,), (1,)), ((), ())), preferred_element_type=F32)
@@ -154,7 +194,9 @@
             ia, ib = xa + da - 2 * xa * da, xb + db - 2 * xb * db
             lo, hi = left(ia, ib)
             cs[e, d] = (outer(lo, right(0, oth)) + outer(hi, right(1, oth))).astype(BF)
-            acc[e, d] = outer(lo, right(0, k)) + outer(hi, right(1, k))
+            keep = outer(lo, right(0, k)) + outer(hi, right(1, k))
+            ac0[e, d] = keep[:, :256]
+            ac1[e, d] = keep[:, 256:].reshape(2, 8, 2, 8, 256)
             return carry
 
         lax.fori_loop(0, 4, one, 0)
@@ -176,48 +218,71 @@
             lambda m, h: x2[0, m, half(h), :],
         )
 
-    xsend, ysend, zsend, csend = {}, {}, {}, {}
-
-    def stage_x(e):
+    xsend, ysend, ysend2, xsend2, zsend, csend = {}, {}, {}, {}, {}, {}
+
+    def push(table, e, d, src, dst, send, recv, to):
+        table[e, d] = remote(src.at[e, d - 1], dst.at[e, d - 1], send.at[e, d - 1], recv.at[e, d - 1], to)
+        table[e, d].start()
+
+    def wait_all(table, e):
         for d in (1, 2, 3):
+            table[e, d].wait_recv()
+
+    def rows_of(d):
+        return flip(yh, d & 2), flip(yl, d & 1)
+
+    def stage_one(e):
+        for d in (2, 1, 3, 0):
             pairs[e, d].wait_recv()
-            xs[e, d - 1] = (acc[e, d] + cr[e, d].astype(F32)).astype(BF)
-            xsend[e, d] = remote(xs.at[e, d - 1], xr.at[e, d - 1], xs_s.at[e, d - 1], xs_r.at[e, d - 1], peer(dx=d))
-            xsend[e, d].start()
-        pairs[e, 0].wait_recv()
-
-    def stage_y(e):
-        for d in (1, 2, 3):
-            xsend[e, d].wait_recv()
-
-        def gather_rows(t, carry):
-            rows = pl.ds(pl.multiple_of(t * 16, 16), 16)
-            total = acc[e, 0, rows, :] + cr[e, 0, rows, :].astype(F32)
+            first_half = ac0[e, d] + cr[e, d, :, :256].astype(F32)
+            if d:
+                xs[e, d - 1] = first_half.astype(BF)
+                push(xsend, e, d, xs, xr, xs_s, xs_r, peer(dx=d))
+            else:
+                ac0[e, 0] = first_half
+            ac1[e, d] += cr[e, d, :, 256:].astype(F32).reshape(2, 8, 2, 8, 256)
+        for d in (2, 1, 3):
+            a, b = rows_of(d)
+            for i in range(4):
+                ys[e, d - 1, i] = ac1[e, i, a, :, b].reshape(64, 256).astype(BF)
+            push(ysend, e, d, ys, yr, ys_s, ys_r, peer(dy=d))
+
+    def stage_two(e):
+        wait_all(xsend, e)
+        total = ac0[e, 0]
+        for j in range(3):
+            total = total + xr[e, j].astype(F32)
+        mid[e] = total.reshape(2, 8, 2, 8, 256)
+        for d in (2, 1, 3):
+            a, b = rows_of(d)
+            ys2[e, d - 1] = mid[e, a, :, b].reshape(64, 256).astype(BF)
+            push(ysend2, e, d, ys2, yr2, ys2_s, ys2_r, peer(dy=d))
+        wait_all(ysend, e)
+        for d in (2, 1, 3, 0):
+            total = ac1[e, d, yh, :, yl].reshape(64, 256)
             for j in range(3):
-                total = total + xr[e, j, rows, :].astype(F32)
-            y, z = lax.div(t, 8), lax.rem(t, 8)
-            yb[e, y * 2, z] = total[:8]
-            yb[e, y * 2 + 1, z] = total[8:]
-            return carry
-
-        lax.fori_loop(0, 16, gather_rows, 0)
-        for d in (2, 1, 3):
-            ysend[e, d] = remote(
-                yb.at[e, flip(yh, d & 2) * 2 + flip(yl, d & 1)],
-                yr.at[e, d - 1],
-                ys_s.at[e, d - 1],
-                ys_r.at[e, d - 1],
-                peer(dy=d),
-            )
-            ysend[e, d].start()
+                total = total + yr[e, j, d].astype(F32)
+            if d:
+                xs2[e, d - 1] = total.astype(BF)
+                push(xsend2, e, d, xs2, xr2, xs2_s, xs2_r, peer(dx=d))
+            else:
+                zb[e, :, 8:, :] = total.reshape(8, 8, 256)
 
     def stage_z(e):
-        for d in (1, 2, 3):
-            ysend[e, d].wait_recv()
-        zb[e] = yb[e, yh * 2 + yl] + yr[e, 0] + yr[e, 1] + yr[e, 2]
+        wait_all(ysend2, e)
+        total = mid[e, yh, :, yl].reshape(64, 256)
+        for j in range(3):
+            total = total + yr2[e, j].astype(F32)
+        zb[e, :, :8, :] = total.reshape(8, 8, 256)
+        wait_all(xsend2, e)
+        total = zb[e, :, 8:, :].reshape(64, 256)
+        for j in range(3):
+            total = total + xr2[e, j].astype(F32)
+        zb[e, :, 8:, :] = total.reshape(8, 8, 256)
+        zs[e] = zb[e].astype(BF)
         for d in (4, 5, 3, 6, 2, 7, 1):
             zsend[e, d] = remote(
-                zb.at[e, (flip(zh, d & 4) * 2 + flip(zm, d & 2)) * 2 + flip(zl, d & 1)],
+                zs.at[e, (flip(zh, d & 4) * 2 + flip(zm, d & 2)) * 2 + flip(zl, d & 1)],
                 zr.at[e, d - 1],
                 zs_s.at[e, d - 1],
                 zs_r.at[e, d - 1],
@@ -230,9 +295,11 @@
             zsend[e, d].wait_recv()
         total = zb[e, (zh * 2 + zm) * 2 + zl]
         for d in range(7):
-            total = total + zr[e, d]
+            total = total + zr[e, d].astype(F32)
+        total = total * scale
         for j in range(4):
-            fb[e, j * 8 : j * 8 + 8, :] = total[:, j * 128 : j * 128 + 128] * scale
+            q, c = j // 2, j % 2
+            fb[e, j * 8 : j * 8 + 8, :] = total[q * 8 : q * 8 + 8, c * 128 : c * 128 + 128]
         for j in range(4):
             lc[e, j * 4 : j * 4 + 4, :] = fb[e, pl.ds(j * 8 + oth * 4, 4), :]
             env_outs[e][pl.ds(k * 4 + j, 4, stride=8), :] = fb[e, pl.ds(j * 8 + k * 4, 4), :]
@@ -244,21 +311,45 @@
         for j in range(4):
             env_outs[e][pl.ds(oth * 4 + j, 4, stride=8), :] = lr[e, j * 4 : j * 4 + 4, :]
 
+    gather(0, -1)
+    gather(1, -1)
     loads[0].wait()
-    gather(0)
+    gather(0, 2)
+    gather(0, 0)
+    gather(0, 1)
     gate_one(0)
-    gate_two(0)
-    gather(1)
+    swapped(0)
+    gate_two(0, 1)
+    close(0, 0, 1, 0)
+    close(0, 0, 1, 1)
+    close_leg(0)
+    gate_two(0, 0)
+    for r, d in ((1, 0), (1, 1), (0, 1), (0, 0)):
+        close(0, r, 0, d)
+    gather(1, 2)
+    close_relay(0, 0)
+    close_relay(0, 1)
+    gather(1, 0)
+    gather(1, 1)
     gate_one(1)
     env_one()
-    gate_two(1)
+    swapped(1)
+    gate_two(1, 1)
+    close(1, 0, 1, 0)
+    close(1, 0, 1, 1)
+    close_leg(1)
+    gate_two(1, 0)
+    stage_one(0)
     env_two()
-    stage_x(0)
-    stage_x(1)
-    stage_y(0)
+    close_relay(1, 0)
+    stage_one(1)
+    stage_two(0)
+    stage_two(1)
+    for r, d in ((1, 0), (1, 1), (0, 1), (0, 0)):
+        close(1, r, 0, d)
     stage_z(0)
-    stage_y(1)
     stage_z(1)
+    close_relay(1, 1)
     stage_core(0)
     stage_core(1)
     stage_end(0)
@@ -267,7 +358,7 @@
         one.wait_recv()
     for one in homes:
         one.wait()
-    for sent in (first, swaps, last, pairs, xsend, ysend, zsend, csend):
+    for sent in (first, relays, relays2, swaps, last, pairs, xsend, ysend, ysend2, xsend2, zsend, csend):
         for one in sent.values():
             one.wait_send()
 
@@ -280,26 +371,35 @@
     scratch = [
         ((1024, 1024), BF),
         ((2, 4, 1024, 128), BF),
+        ((2, 1024, 128), BF),
+        ((2, 2, 256, 256), BF),
         ((1024, 128), F32),
         ((2, 2, 1024, 256), BF),
         ((2, 2, 1024, 256), BF),
         ((2, 4, 256, 256), BF),
         ((2, 2, 1024, 256), BF),
-        ((2, 4, 256, 512), F32),
+        ((2, 4, 256, 256), F32),
+        ((2, 4, 2, 8, 2, 8, 256), F32),
+        ((2, 2, 8, 2, 8, 256), F32),
         ((2, 4, 256, 512), BF),
         ((2, 4, 256, 512), BF),
-        ((2, 3, 256, 512), BF),
-        ((2, 3, 256, 512), BF),
-        ((2, 4, 8, 8, 512), F32),
-        ((2, 3, 8, 8, 512), F32),
-        ((2, 8, 8, 512), F32),
-        ((2, 7, 8, 512), F32),
+        ((2, 3, 256, 256), BF),
+        ((2, 3, 256, 256), BF),
+        ((2, 3, 4, 64, 256), BF),
+        ((2, 3, 4, 64, 256), BF),
+        ((2, 3, 64, 256), BF),
+        ((2, 3, 64, 256), BF),
+        ((2, 3, 64, 256), BF),
+        ((2, 3, 64, 256), BF),
+        ((2, 8, 16, 256), F32),
+        ((2, 8, 16, 256), BF),
+        ((2, 7, 16, 256), BF),
         ((2, 32, 128), F32),
         ((2, 16, 128), F32),
         ((2, 16, 128), F32),
     ]
     sems = [(3,), (2,)]
-    for shape in ((2, 3), (2, 4), (2, 7), (2, 4), (2, 3), (2, 3), (2, 7), (2,)):
+    for shape in ((2, 3), (2,), (2, 2), (2, 4), (2, 7), (2, 4), (2, 3), (2, 3), (2, 3), (2, 3), (2, 7), (2,)):
         sems += [shape, shape]
     outs = pl.pallas_call(
         lambda *refs: kernel(scale, *refs),

time: 136 us -> 121 us (0.89)
  Pallas kernels: 129 us -> 113 us
    pallas_call x1, Pallas kernels: 129 us -> 113 us  [on_device(): pl.pallas_call(lambda *refs: kernel(scale, *refs), out_shape=[jax.ShapeDt...]
where the time goes in v2:
time: 121 us; the launch traced here: 119 us
  Pallas kernels  113 us (93%)
  local copies, waits for them, and re-layouts  5.31 us (4%)
    pallas_call x1, Pallas kernels, on_device(): pl.pallas_call(lambda *refs: kernel(scale, *refs), out_shape=[jax.ShapeDt...  113 us
    unnamed x10, local copies, waits for them, and re-layouts  5.31 us

profile of v2, /device:TPU:33, one launch (start us, length us, event | category | flops | bytes accessed | tf_op | source)
XLA Modules:
  0.0 119.4 jit_solution(1143752862295601436)
XLA Ops:
  0.6 113.4 %step.1 = (bf16[4,256,512]{2,1,0:T(8,128)(2,1)}, bf16[4,256,512]{2,1,0:T(8,128)(2,1)}, f32[32,128]{1,0:T(8,128)}, f32[32,128]{1,0:T(8,128)}) custom-call(bf16[4,1024,128]{2,1,0:T(8,128)(2,1)} %bitcast.12, bf16[4,1024,128]{2,1,0:T(8,128)(2,1)} %bitcast.13, bf16[1024,1024]{1,0:T(8,128)(2,1)} %refs_2_.1), custom_call_target="tpu_custom_call" | custom-call | tf_op jit(solution)/shard_map/step/pallas_call | solution.py:404
  114.0 0.0 copy-start
  114.0 0.0 copy-start.2
  114.0 0.0 copy-start.1
  114.0 2.7 %copy.7 = bf16[128,4,8,128]{3,1,2,0:T(4,128)(2,1)} copy(bf16[128,4,8,128]{3,2,1,0:T(8,128)(2,1)} %bitcast.11) | data formatting | bytes 2097152
  116.7 0.0 copy-done
  116.7 1.4 %copy.8 = bf16[128,4,8,128]{3,1,2,0:T(4,128)(2,1)} copy(bf16[128,4,8,128]{3,2,1,0:T(8,128)(2,1)S(1)} %bitcast.10) | data formatting | bytes 2097152
  118.1 0.0 copy-done.2
  118.1 0.6 copy.11
  118.7 0.0 copy-done.1
  118.7 0.6 copy.12
Async XLA Ops:
  114.0 2.7 %copy-start = (bf16[4,256,512]{2,1,0:T(8,128)(2,1)S(1)}, bf16[4,256,512]{2,1,0:T(8,128)(2,1)}, u32[]{:S(2)}) copy-start(bf16[4,256,512]{2,1,0:T(8,128)(2,1)} %get-tuple-element.9) | copy-start | bytes 3145732
  114.0 4.1 %copy-start.2 = (f32[32,128]{1,0:T(8,128)S(1)}, f32[32,128]{1,0:T(8,128)}, u32[]{:S(2)}) copy-start(f32[32,128]{1,0:T(8,128)} %get-tuple-element.10) | copy-start | bytes 49156
  114.0 4.7 %copy-start.1 = (f32[32,128]{1,0:T(8,128)S(1)}, f32[32,128]{1,0:T(8,128)}, u32[]{:S(2)}) copy-start(f32[32,128]{1,0:T(8,128)} %get-tuple-element.11) | copy-start | bytes 49156

commit v3 on v2

--- a/solution.py
+++ b/solution.py
@@ -45,7 +45,7 @@
     home = yh * 2 + zh
 
     group = [(r, c, d) for r in (0, 1) for c in (1, 0) for d in (0, 1) if r + c + d]
-    friends = [peer(dy=2 * r, dz=4 * c, dk=d) for r, c, d in group]
+    friends = [peer(dy=2 * r, dz=4 * c, dk=d) for r, c, d in group if r + c < 2]
     friends += [peer(dx=d) for d in (1, 2, 3)] + [peer(dy=d) for d in (1, 3)]
     friends += [peer(dz=d) for d in (1, 2, 3, 5, 6, 7)]
     barrier = pltpu.get_barrier_semaphore()
@@ -86,8 +86,8 @@
     open_leg(1)
     open_direct(0, 2)
     open_direct(1, 2)
+    open_direct(1, 0)
     open_relay(0)
-    open_direct(1, 0)
     open_relay(1)
 
     def untangle(s, slot):
@@ -361,6 +361,31 @@
     for sent in (first, relays, relays2, swaps, last, pairs, xsend, ysend, ysend2, xsend2, zsend, csend):
         for one in sent.values():
             one.wait_send()
+
+
+def lay_out(f_in, a_in, e1_in, e2_in, f_out, a_out, e1_out, e2_out, grid, tmp, flat, env, in_sem, out_sem):
+    ins, outs = [], []
+    for s, ref in enumerate((f_in, a_in)):
+        for p in range(4):
+            ins.append(pltpu.make_async_copy(ref.at[p], grid.at[s, p], in_sem.at[s * 4 + p]))
+    for e, ref in enumerate((e1_in, e2_in)):
+        ins.append(pltpu.make_async_copy(ref, env.at[e], in_sem.at[8 + e]))
+    for one in ins:
+        one.start()
+    for s, ref in enumerate((f_out, a_out)):
+        for p in range(4):
+            ins[s * 4 + p].wait()
+            for m in range(4):
+                tmp[p % 2, pl.ds(m, 256, stride=4), :] = grid[s, p, :, m * 128 : m * 128 + 128].astype(F32)
+            flat[s, p] = tmp[p % 2].astype(BF)
+            outs.append(pltpu.make_async_copy(flat.at[s, p], ref.at[p], out_sem.at[s * 4 + p]))
+            outs[-1].start()
+    for e, ref in enumerate((e1_out, e2_out)):
+        ins[8 + e].wait()
+        outs.append(pltpu.make_async_copy(env.at[e], ref, out_sem.at[8 + e]))
+        outs[-1].start()
+    for one in outs:
+        one.wait()
 
 
 def on_device(forward_state, adjoint_state, gate_matrix):
@@ -415,6 +440,21 @@
         compiler_params=pltpu.CompilerParams(collective_id=0, has_side_effects=True),
         name="step",
     )(forward_state.reshape(4, 1024, 128), adjoint_state.reshape(4, 1024, 128), gate_matrix)
+    outs = pl.pallas_call(
+        lay_out,
+        out_shape=[jax.ShapeDtypeStruct((4, 1024, 128), BF)] * 2 + [jax.ShapeDtypeStruct((32, 128), F32)] * 2,
+        in_specs=[any_space] * 4,
+        out_specs=[any_space] * 4,
+        scratch_shapes=[
+            pltpu.VMEM((2, 4, 256, 512), BF),
+            pltpu.VMEM((2, 1024, 128), F32),
+            pltpu.VMEM((2, 4, 1024, 128), BF),
+            pltpu.VMEM((2, 32, 128), F32),
+            dma((10,)),
+            dma((10,)),
+        ],
+        name="lay_out",
+    )(*outs)
     return tuple(one.reshape(-1) for one in outs)
 
 

time: 121 us -> 112 us (0.926)
  local copies, waits for them, and re-layouts: 5.31 us -> 0 us
  Pallas kernels: 113 us -> 111 us
    unnamed x10 -> x0, local copies, waits for them, and re-layouts: 5.31 us -> none
    pallas_call x1, Pallas kernels: 113 us -> 108 us  [on_device(): pl.pallas_call(lambda *refs: kernel(scale, *refs), out_shape=[jax.ShapeDt...]
    pallas_call x0 -> x1, Pallas kernels: none -> 2.54 us  [on_device(): pl.pallas_call(lay_out, out_shape=[jax.ShapeDtypeStruct((4, 1024, 128), B...]
where the time goes in v3:
time: 112 us
  Pallas kernels  111 us (99%)
    pallas_call x1, Pallas kernels, on_device(): pl.pallas_call(lambda *refs: kernel(scale, *refs), out_shape=[jax.ShapeDt...  108 us
    pallas_call x1, Pallas kernels, on_device(): pl.pallas_call(lay_out, out_shape=[jax.ShapeDtypeStruct((4, 1024, 128), B...  2.54 us

profile of v3, /device:TPU:33, one launch (start us, length us, event | category | flops | bytes accessed | tf_op | source)
XLA Modules:
  0.0 111.5 jit_solution(15861819152650710951)
XLA Ops:
  0.6 108.4 %step.1 = (bf16[4,256,512]{2,1,0:T(8,128)(2,1)}, bf16[4,256,512]{2,1,0:T(8,128)(2,1)}, f32[32,128]{1,0:T(8,128)}, f32[32,128]{1,0:T(8,128)}) custom-call(bf16[4,1024,128]{2,1,0:T(8,128)(2,1)} %bitcast.6, bf16[4,1024,128]{2,1,0:T(8,128)(2,1)} %bitcast.7, bf16[1024,1024]{1,0:T(8,128)(2,1)} %refs_2_.1), custom_call_target="tpu_custom_call" | custom-call | tf_op jit(solution)/shard_map/step/pallas_call | solution.py:429
  109.0 2.5 %lay_out.1 = (bf16[4,1024,128]{2,1,0:T(8,128)(2,1)}, bf16[4,1024,128]{2,1,0:T(8,128)(2,1)}, f32[32,128]{1,0:T(8,128)}, f32[32,128]{1,0:T(8,128)}) custom-call(bf16[4,256,512]{2,1,0:T(8,128)(2,1)} %get-tuple-element.12.f_in, bf16[4,256,512]{2,1,0:T(8,128)(2,1)} %get-tuple-element.13.a_in, f32[32,128]{1,0:T(8,128)} %get-tuple-element.14.e1_in, ...), custom_call_target="tpu_custom_call" | custom-call | tf_op jit(solution)/shard_map/lay_out/pallas_call | solution.py:443

commit v4 on v3

--- a/solution.py
+++ b/solution.py
@@ -434,12 +434,16 @@
             jax.ShapeDtypeStruct((32, 128), F32),
             jax.ShapeDtypeStruct((32, 128), F32),
         ],
-        in_specs=[any_space] * 3,
+        in_specs=[pl.BlockSpec(memory_space=pltpu.HBM)] * 3,
         out_specs=[any_space, any_space, vmem, vmem],
         scratch_shapes=[pltpu.VMEM(shape, kind) for shape, kind in scratch] + [dma(shape) for shape in sems],
-        compiler_params=pltpu.CompilerParams(collective_id=0, has_side_effects=True),
+        compiler_params=pltpu.CompilerParams(collective_id=0, has_side_effects=True, vmem_limit_bytes=36 << 20),
         name="step",
-    )(forward_state.reshape(4, 1024, 128), adjoint_state.reshape(4, 1024, 128), gate_matrix)
+    )(
+        pltpu.with_memory_space_constraint(forward_state.reshape(4, 1024, 128), pltpu.HBM),
+        pltpu.with_memory_space_constraint(adjoint_state.reshape(4, 1024, 128), pltpu.HBM),
+        pltpu.with_memory_space_constraint(gate_matrix, pltpu.HBM),
+    )
     outs = pl.pallas_call(
         lay_out,
         out_shape=[jax.ShapeDtypeStruct((4, 1024, 128), BF)] * 2 + [jax.ShapeDtypeStruct((32, 128), F32)] * 2,
@@ -453,6 +457,7 @@
             dma((10,)),
             dma((10,)),
         ],
+        compiler_params=pltpu.CompilerParams(vmem_limit_bytes=16 << 20),
         name="lay_out",
     )(*outs)
     return tuple(one.reshape(-1) for one in outs)

time: 112 us -> 110 us (0.982)
  Pallas kernels: 111 us -> 109 us
where the time goes in v4:
time: 110 us
  Pallas kernels  109 us (99%)
    pallas_call x1, Pallas kernels, on_device(): pl.pallas_call(lambda *refs: kernel(scale, *refs), out_shape=[jax.ShapeDt...  108 us

profile of v4, /device:TPU:33, one launch (start us, length us, event | category | flops | bytes accessed | tf_op | source)
XLA Modules:
  0.0 110.1 jit_solution(2389331521708434441)
XLA Ops:
  0.6 107.6 %step.1 = (bf16[4,256,512]{2,1,0:T(8,128)(2,1)S(1)}, bf16[4,256,512]{2,1,0:T(8,128)(2,1)S(1)}, f32[32,128]{1,0:T(8,128)S(1)}, f32[32,128]{1,0:T(8,128)S(1)}) custom-call(bf16[4,1024,128]{2,1,0:T(8,128)(2,1)} %bitcast.6, bf16[4,1024,128]{2,1,0:T(8,128)(2,1)} %bitcast.7, bf16[1024,1024]{1,0:T(8,128)(2,1)} %refs_2_.1), custom_call_target="tpu_custom_call" | custom-call | tf_op jit(solution)/shard_map/step/pallas_call | solution.py:429
  108.3 1.8 %lay_out.1 = (bf16[4,1024,128]{2,1,0:T(8,128)(2,1)}, bf16[4,1024,128]{2,1,0:T(8,128)(2,1)}, f32[32,128]{1,0:T(8,128)}, f32[32,128]{1,0:T(8,128)}) custom-call(bf16[4,256,512]{2,1,0:T(8,128)(2,1)S(1)} %get-tuple-element.12.f_in, bf16[4,256,512]{2,1,0:T(8,128)(2,1)S(1)} %get-tuple-element.13.a_in, f32[32,128]{1,0:T(8,128)S(1)} %get-tuple-element.14.e1_in, ...), custom_call_target="tpu_custom_call" | custom-call | tf_op jit(solution)/shard_map/lay_out/pallas_call | solution.py:447
